TPU v7x, 32 devices: a whole 2x2x4 slice. The times are simulated.
32 devices in a mesh: fsdp: 8 (over y, x, core), sp: 4 (over z).
Axes of the slice: x: 2, y: 2, z: 4, core: 2. Of those that a mesh axis runs over, the one named last changes fastest.
Arguments:
- hidden_in: bfloat16 [8, 1024, 2048], P('fsdp', 'sp'), may hold values from -6 to 6
- segments: int32 [8, 1024], P('fsdp'), may hold values from 0 to 3, never falling along the last dimension, each value on 1 to 640 neighbouring positions
- ln1_gain: float32 [2048], replicated, may hold values from 0.5 to 1.5
- ln1_bias: float32 [2048], replicated, may hold values from -1 to 1
- ln2_gain: float32 [2048], replicated, may hold values from 0.5 to 1.5
- ln2_bias: float32 [2048], replicated, may hold values from -1 to 1
- w_qkv: bfloat16 [6144, 2048], P('fsdp'), may hold values from -0.125 to 0.125
- b_qkv: float32 [6144], replicated, may hold values from -1 to 1
- w_dense: bfloat16 [2048, 2048], P('fsdp'), may hold values from -0.75 to 0.75
- b_dense: float32 [2048], replicated, may hold values from -1 to 1
- w_up: bfloat16 [8192, 2048], P('fsdp'), may hold values from -0.125 to 0.125
- b_up: float32 [8192], replicated, may hold values from -1 to 1
- w_down: bfloat16 [8192, 2048], P('fsdp'), may hold values from -0.0625 to 0.0625
- b_down: float32 [2048], replicated, may hold values from -1 to 1
- cotangent: bfloat16 [8, 1024, 2048], P('fsdp', 'sp'), may hold values from -6 to 6
Outputs:
- output: bfloat16 [8, 1024, 2048], P('fsdp', 'sp')
- input_grad: bfloat16 [8, 1024, 2048], P('fsdp', 'sp')
- grad_ln1_gain: float32 [2048], P('fsdp')
- grad_ln1_bias: float32 [2048], P('fsdp')
- grad_ln2_gain: float32 [2048], P('fsdp')
- grad_ln2_bias: float32 [2048], P('fsdp')
- grad_w_qkv: float32 [6144, 2048], P('fsdp')
- grad_b_qkv: float32 [6144], P('fsdp')
- grad_w_dense: float32 [2048, 2048], P('fsdp')
- grad_b_dense: float32 [2048], P('fsdp')
- grad_w_up: float32 [8192, 2048], P('fsdp')
- grad_b_up: float32 [8192], P('fsdp')
- grad_w_down: float32 [8192, 2048], P('fsdp')
- grad_b_down: float32 [2048], P('fsdp')
Inputs may be any that keep to these rules, and one draw needn't show every extreme that they name: `segments`: along each sequence the segment numbers never fall; each document is one run of 1 to 640 positions, and some document has exactly 640.
All inputs are finite; a program needn't handle non-finite values.
Results may differ from a plain program's by a relative error of at most 0.011.
Values may be sent and summed in bfloat16 or wider, within the bound.
A program may use at most 704 MiB of HBM per device.

v0:
```python
import math
import jax
import jax.numpy as jnp
from jax import lax
from jax.sharding import PartitionSpec as P

HEADS = 8
HEAD_DIM = 256
ROT = 64
EPSILON = 1e-05
NEGATIVE = -1e30
ROOT_HALF = 0.7071067811865476
ROOT_TWO_PI = 2.5066282746310002
SCALE = 1.0 / math.sqrt(HEAD_DIM)


def rounded(array):
    return lax.reduce_precision(array.astype(jnp.float32), 8, 7).astype(jnp.bfloat16)


def contract_rows(former, latter):
    return lax.dot_general(
        former, latter, (((0,), (0,)), ((), ())), preferred_element_type=jnp.float32
    )


def times_transposed(former, latter):
    return lax.dot_general(
        former, latter, (((1,), (1,)), ((), ())), preferred_element_type=jnp.float32
    )


def times(former, latter):
    return jnp.dot(former, latter, preferred_element_type=jnp.float32)


def norm_scaled(inputs):
    average = jnp.mean(inputs, axis=-1, keepdims=True)
    centred = inputs - average
    variance = jnp.mean(centred * centred, axis=-1, keepdims=True)
    inverse = lax.rsqrt(variance + EPSILON)
    return (centred * inverse, inverse)


def gelu_pair(hidden):
    cumulative = 0.5 * (1.0 + jax.scipy.special.erf(hidden * ROOT_HALF))
    return (
        hidden * cumulative,
        cumulative + hidden * jnp.exp(-0.5 * hidden * hidden) / ROOT_TWO_PI,
    )


def rotary_tables(segment_rows):
    length = segment_rows.shape[-1]
    places = jnp.arange(length, dtype=jnp.int32)
    changes = jnp.concatenate(
        [
            jnp.ones_like(segment_rows[..., :1]),
            (segment_rows[..., 1:] != segment_rows[..., :-1]).astype(jnp.int32),
        ],
        axis=-1,
    )
    first_place = lax.cummax(changes * places, axis=segment_rows.ndim - 1)
    position = (places - first_place).astype(jnp.float32)
    exponent = jnp.arange(0, ROT, 2).astype(jnp.float32) / ROT
    frequency = 1.0 / jnp.power(10000.0, exponent)
    angles = position[..., None] * frequency
    angles = jnp.concatenate([angles, angles], axis=-1)
    return (jnp.cos(angles), jnp.sin(angles))


def rotate(heads_part, cos_table, sin_table):
    half_rot = ROT // 2
    turned = heads_part[..., :ROT]
    swapped = jnp.concatenate([-turned[..., half_rot:], turned[..., :half_rot]], axis=-1)
    turned = turned * cos_table[..., None, :] + swapped * sin_table[..., None, :]
    return jnp.concatenate([turned, heads_part[..., ROT:]], axis=-1)


def unrotate(grads_part, cos_table, sin_table):
    half_rot = ROT // 2
    turned = grads_part[..., :ROT]
    along_sin = turned * sin_table[..., None, :]
    back_turn = jnp.concatenate([along_sin[..., half_rot:], -along_sin[..., :half_rot]], axis=-1)
    turned = turned * cos_table[..., None, :] + back_turn
    return jnp.concatenate([turned, grads_part[..., ROT:]], axis=-1)


def build_mask(segment_rows):
    places = jnp.arange(segment_rows.shape[-1], dtype=jnp.int32)
    return (segment_rows[:, :, None] == segment_rows[:, None, :]) & (
        places[None, :] <= places[:, None]
    )


def attention_scores(queries, keys_rot):
    return (
        jnp.einsum("bqhd,bkhd->bhqk", queries, keys_rot, preferred_element_type=jnp.float32) * SCALE
    )


def attend_forward(queries, keys_rot, values, mask):
    scores = jnp.where(mask[:, None], attention_scores(queries, keys_rot), NEGATIVE)
    row_top = jnp.max(scores, axis=-1, keepdims=True)
    exponent = jnp.exp(scores - row_top)
    row_total = jnp.sum(exponent, axis=-1, keepdims=True)
    attention = (exponent / row_total).astype(jnp.bfloat16)
    context = jnp.einsum("bhqk,bkhd->bqhd", attention, values, preferred_element_type=jnp.float32)
    return (context.astype(jnp.bfloat16), row_top + jnp.log(row_total))


def attend_backward(queries, keys_rot, values, mask, log_total, context_grad):
    scores = attention_scores(queries, keys_rot)
    attention = jnp.where(mask[:, None], jnp.exp(scores - log_total), 0.0)
    value_grad = jnp.einsum(
        "bhqk,bqhd->bkhd",
        attention.astype(jnp.bfloat16),
        context_grad,
        preferred_element_type=jnp.float32,
    )
    attention_grad = jnp.einsum(
        "bqhd,bkhd->bhqk", context_grad, values, preferred_element_type=jnp.float32
    )
    row_centre = jnp.sum(attention * attention_grad, axis=-1, keepdims=True)
    score_grad = (attention * (attention_grad - row_centre)).astype(jnp.bfloat16)
    query_grad = (
        jnp.einsum("bhqk,bkhd->bqhd", score_grad, keys_rot, preferred_element_type=jnp.float32)
        * SCALE
    )
    key_grad = (
        jnp.einsum("bhqk,bqhd->bkhd", score_grad, queries, preferred_element_type=jnp.float32)
        * SCALE
    )
    return (query_grad, key_grad, value_grad)


def sum_over_line(partial):
    inward = lax.ppermute(partial, "sp", [(0, 1), (3, 2)])
    half = rounded(partial.astype(jnp.float32) + inward.astype(jnp.float32))
    other = lax.ppermute(half, "sp", [(1, 2), (2, 1)])
    whole = rounded(half.astype(jnp.float32) + other.astype(jnp.float32))
    outward = lax.ppermute(whole, "sp", [(1, 0), (2, 3)])
    place = lax.axis_index("sp")
    inner = (place == 1) | (place == 2)
    return jnp.where(inner, whole, outward).astype(jnp.float32)


def sum_over_sp(partial):
    partial = rounded(partial)
    if lax.axis_size("sp") == 4:
        return sum_over_line(partial)
    return lax.psum(partial, "sp").astype(jnp.float32)


def per_device(
    hidden_in,
    segments,
    ln1_gain,
    ln1_bias,
    ln2_gain,
    ln2_bias,
    w_qkv,
    b_qkv,
    w_dense,
    b_dense,
    w_up,
    b_up,
    w_down,
    b_down,
    cotangent,
):
    seq_local, shard_len, width = hidden_in.shape
    seq_len = segments.shape[1]
    nf, ns = (lax.axis_size("fsdp"), lax.axis_size("sp"))
    f_place, s_place = (lax.axis_index("fsdp"), lax.axis_index("sp"))
    seqs = seq_local * nf
    group = seqs // ns
    piece = shard_len // nf
    tokens = group * seq_len
    per_head = max(1, nf // HEADS)
    head_count = max(1, HEADS // nf)
    head_sets = [[head * per_head + k for k in range(per_head)] for head in range(nf // per_head)]

    def gather_tokens(block):
        part = lax.all_to_all(block, "fsdp", split_axis=1, concat_axis=0, tiled=True)
        part = lax.all_to_all(part, "sp", split_axis=0, concat_axis=1, tiled=True)
        return lax.all_gather(part, "fsdp", axis=0, tiled=True).reshape(tokens, width)

    def scatter_tokens(partial):
        part = partial.reshape(nf * group, ns * piece, width)
        part = lax.psum_scatter(part, "fsdp", scatter_dimension=0, tiled=True)
        part = lax.all_to_all(part, "sp", split_axis=1, concat_axis=0, tiled=True)
        return lax.all_to_all(part, "fsdp", split_axis=0, concat_axis=1, tiled=True)

    def in_order(array):
        array = array.reshape(nf, group, ns, piece, -1)
        return array.transpose(1, 2, 0, 3, 4).reshape(group, seq_len, -1)

    def out_of_order(array):
        array = array.reshape(group, ns, nf, piece, -1)
        return array.transpose(2, 0, 1, 3, 4).reshape(tokens, -1)

    def over_head(array, axis):
        if per_head == 1:
            return array
        return lax.all_gather(array, "fsdp", axis=axis, tiled=True, axis_index_groups=head_sets)

    def own_columns(array):
        if per_head == 1:
            return array
        share = array.shape[-1] // per_head
        return lax.dynamic_slice_in_dim(array, f_place % per_head * share, share, array.ndim - 1)

    def own_part(vector):
        share = vector.shape[0] // nf
        return lax.dynamic_slice_in_dim(vector, f_place * share, share, 0)

    gathered = gather_tokens(hidden_in)
    upstream = gather_tokens(cotangent)
    rows = lax.all_gather(segments, "fsdp", axis=0, tiled=True)
    rows = lax.dynamic_slice_in_dim(rows, s_place * group, group, 0)
    dense_in = lax.all_to_all(w_dense, "fsdp", split_axis=1, concat_axis=0, tiled=True)
    head_qkv = over_head(w_qkv, 0)
    head_dense = over_head(dense_in, 1)
    head_bias = lax.dynamic_slice_in_dim(
        b_qkv, f_place // per_head * head_qkv.shape[0], head_qkv.shape[0], 0
    )
    scaled, _ = norm_scaled(gathered.astype(jnp.float32))
    normed = (scaled * ln1_gain + ln1_bias).astype(jnp.bfloat16)
    normed_mlp = (scaled * ln2_gain + ln2_bias).astype(jnp.bfloat16)
    hidden = times_transposed(normed_mlp, w_up) + own_part(b_up)
    activated, slope = gelu_pair(hidden)
    activated = activated.astype(jnp.bfloat16)
    hidden_grad = (times_transposed(upstream, w_down) * slope).astype(jnp.bfloat16)
    down_term = contract_rows(activated, upstream)
    up_term = contract_rows(hidden_grad, normed_mlp)
    mlp_norm_grad = times(hidden_grad, w_up)
    packed = (times_transposed(normed, head_qkv) + head_bias).astype(jnp.bfloat16)
    packed = in_order(packed).reshape(group, seq_len, head_count, 3 * HEAD_DIM)
    cos_table, sin_table = rotary_tables(rows)
    queries = rotate(packed[..., :HEAD_DIM].astype(jnp.float32), cos_table, sin_table).astype(
        jnp.bfloat16
    )
    keys_rot = rotate(
        packed[..., HEAD_DIM : 2 * HEAD_DIM].astype(jnp.float32), cos_table, sin_table
    ).astype(jnp.bfloat16)
    values = packed[..., 2 * HEAD_DIM :]
    mask = build_mask(rows)
    context, log_total = attend_forward(queries, keys_rot, values, mask)
    context = own_columns(out_of_order(context))
    partial_out = times_transposed(context, dense_in) + times(activated, w_down)
    context_grad = in_order(times(upstream, head_dense).astype(jnp.bfloat16)).reshape(
        group, seq_len, head_count, HEAD_DIM
    )
    query_grad, key_grad, value_grad = attend_backward(
        queries, keys_rot, values, mask, log_total, context_grad
    )
    packed_grad = jnp.concatenate(
        [
            unrotate(query_grad, cos_table, sin_table),
            unrotate(key_grad, cos_table, sin_table),
            value_grad,
        ],
        axis=-1,
    ).astype(jnp.bfloat16)
    packed_grad = own_columns(out_of_order(packed_grad))
    attn_norm_grad = times(packed_grad, w_qkv)
    qkv_term = contract_rows(packed_grad, normed)
    dense_term = contract_rows(upstream, context).astype(jnp.bfloat16)
    dense_term = lax.all_to_all(dense_term, "fsdp", split_axis=0, concat_axis=1, tiled=True)
    vectors = jnp.stack(
        [
            jnp.sum(attn_norm_grad * scaled, axis=0),
            jnp.sum(attn_norm_grad, axis=0),
            jnp.sum(mlp_norm_grad * scaled, axis=0),
            jnp.sum(mlp_norm_grad, axis=0),
        ],
        axis=1,
    )
    vectors = lax.psum_scatter(vectors, "fsdp", scatter_dimension=0, tiled=True)
    bias_out = own_part(jnp.sum(upstream.astype(jnp.float32), axis=0))
    bias_qkv = jnp.sum(packed_grad.astype(jnp.float32), axis=0)
    bias_up = jnp.sum(hidden_grad.astype(jnp.float32), axis=0)
    vectors, bias_out, bias_qkv, bias_up = lax.psum((vectors, bias_out, bias_qkv, bias_up), "sp")
    output = scatter_tokens(rounded(partial_out))
    weighted = scatter_tokens(rounded(attn_norm_grad * ln1_gain + mlp_norm_grad * ln2_gain))
    inputs = hidden_in.astype(jnp.float32)
    output = (inputs + (output.astype(jnp.float32) + (b_dense + b_down))).astype(jnp.bfloat16)
    own_scaled, own_inverse = norm_scaled(inputs)
    weighted = weighted.astype(jnp.float32)
    first_mean = jnp.mean(weighted, axis=-1, keepdims=True)
    second_mean = jnp.mean(weighted * own_scaled, axis=-1, keepdims=True)
    input_grad = (
        cotangent.astype(jnp.float32)
        + own_inverse * (weighted - first_mean - own_scaled * second_mean)
    ).astype(jnp.bfloat16)
    grad_down_w = sum_over_sp(down_term)
    grad_up_w = sum_over_sp(up_term)
    grad_qkv_w = sum_over_sp(qkv_term)
    grad_dense_w = sum_over_sp(dense_term)
    return (
        output,
        input_grad,
        vectors[:, 0],
        vectors[:, 1],
        vectors[:, 2],
        vectors[:, 3],
        grad_qkv_w,
        bias_qkv,
        grad_dense_w,
        bias_out,
        grad_up_w,
        bias_up,
        grad_down_w,
        bias_out,
    )


def solution(mesh):
    rows = P("fsdp", "sp", None)
    first = P("fsdp", None)
    return jax.shard_map(
        per_device,
        mesh=mesh,
        in_specs=(
            rows,
            first,
            P(),
            P(),
            P(),
            P(),
            first,
            P(),
            first,
            P(),
            first,
            P(),
            first,
            P(),
            rows,
        ),
        out_specs=(
            rows,
            rows,
            P("fsdp"),
            P("fsdp"),
            P("fsdp"),
            P("fsdp"),
            first,
            P("fsdp"),
            first,
            P("fsdp"),
            first,
            P("fsdp"),
            first,
            P("fsdp"),
        ),
        check_vma=False,
    )
```

profile of v0, /device:TPU:0, one launch (start us, length us, event | category | flops | bytes accessed | tf_op | source)
XLA Modules:
  0.0 1062.1 jit_solution(14219116837195556078)
XLA Ops:
  12.1 9.0 reduce.19
  23.7 20.6 %all_to_all.146 = bf16[8,2,32768]{2,1,0:T(2,128)(2,1)} all-to-all(bf16[8,2,32768]{2,1,0:T(2,128)(2,1)} %reshape.579), channel_id=1, replica_groups=mesh['fsdp'=8,'sp'=4] {'fsdp'}, dimensions={0} | all-to-all | bytes 2097152 | tf_op jit(solution)/shard_map/all_to_all | solution.py:185
  52.3 30.2 %all_to_all.147 = bf16[8,32,2048]{2,1,0:T(8,128)(2,1)S(1)} all-to-all(bf16[8,32,2048]{2,1,0:T(8,128)(2,1)S(1)} %bitcast.199), channel_id=1, replica_groups=mesh['fsdp'=8,'sp'=4] {'sp'}, dimensions={0} | all-to-all | bytes 2097152 | tf_op jit(solution)/shard_map/all_to_all | solution.py:186
  88.0 9.2 reduce.20
  99.8 26.8 %all_to_all.148 = bf16[8,2,32768]{2,1,0:T(2,128)(2,1)} all-to-all(bf16[8,2,32768]{2,1,0:T(2,128)(2,1)} %reshape.581), channel_id=1, replica_groups=mesh['fsdp'=8,'sp'=4] {'fsdp'}, dimensions={0} | all-to-all | bytes 2097152 | tf_op jit(solution)/shard_map/all_to_all | solution.py:185
  134.6 26.5 %all_to_all.149 = bf16[8,32,2048]{2,1,0:T(8,128)(2,1)S(1)} all-to-all(bf16[8,32,2048]{2,1,0:T(8,128)(2,1)S(1)} %bitcast.200), channel_id=1, replica_groups=mesh['fsdp'=8,'sp'=4] {'sp'}, dimensions={0} | all-to-all | bytes 2097152 | tf_op jit(solution)/shard_map/all_to_all | solution.py:186
  168.7 26.7 %all-gather = s32[8,1,1024]{2,1,0:T(1,128)S(1)} all-gather(s32[1,1,1024]{2,1,0:T(1,128)S(1)} %bitcast.233), channel_id=1, replica_groups=mesh['fsdp'=8,'sp'=4] {'fsdp'}, dimensions={0}, use_global_device_ids=true | all-gather | bytes 36864 | tf_op jit(solution)/shard_map/all_gather | solution.py:220
  298.7 15.7 %multiply_convert_fusion.1 = (bf16[2048,1024]{1,0:T(8,128)(2,1)}, f32[2048,1024]{1,0:T(8,128)}) fusion(f32[1024]{0:T(1024)S(1)} %dynamic_slice.14, bf16[2048,2048]{1,0:T(8,128)(2,1)} %get-tuple-element.26, bf16[1024,2048]{1,0:T(8,128)(2,1)S(1)} %copy-done.39), kind=kOutput, calls=%fused_computation.29 | convolution fusion | flops 8602517504 | bytes 25169920 | tf_op jit(solution)/shard_map/dot_general | solution.py:28
  314.4 17.5 %convert_reduce_fusion.2 = (f32[1024]{0:T(1024)}, bf16[2048,1024]{1,0:T(8,128)(2,1)}) fusion(f32[2048,1024]{1,0:T(8,128)} %get-tuple-element.60, f32[1024]{0:T(1024)S(1)} %dynamic_slice.14, bf16[2048,2048]{1,0:T(8,128)(2,1)S(1)} %bitcast.176, bf16[1024,2048]{1,0:T(8,128)(2,1)} %param.27), kind=kOutput, calls=%fused_computation.22 | convolution fusion | flops 8617196544 | bytes 25174016 | tf_op jit(solution)/shard_map/dot_general | solution.py:28
  331.9 14.1 %fusion.59 = f32[2048,2048]{1,0:T(8,128)} fusion(bf16[2048,1024]{1,0:T(8,128)(2,1)} %get-tuple-element.62, bf16[1024,2048]{1,0:T(8,128)(2,1)S(1)} %copy-done.39), kind=kOutput, calls=%fused_computation.148 | convolution fusion | flops 8589934592 | bytes 25165824 | tf_op jit(solution)/shard_map/dot_general | solution.py:34
  346.0 17.8 %multiply_reduce_fusion.1 = (f32[2048]{0:T(1024)S(1)}, f32[2048]{0:T(1024)S(1)}, f32[2048]{0:T(1024)S(1)}, f32[2048]{0:T(1024)S(1)}, bf16[2048,2048]{1,0:T(8,128)(2,1)}) fusion(bf16[16,128,2048]{2,1,0:T(8,128)(2,1)} %all-gather.4.cloned.1.call-done, f32[2048]{0:T(1024)S(1)} %get-tuple-element.48, f32[2048]{0:T(1024)S(1)} %get-tuple-element.49, ...), kind=kOutput, calls=%fused_computation.5 | convolution fusion | flops 6501163008 | bytes 39911424 | tf_op jit(solution)/shard_map/dot_general | solution.py:34
  373.6 15.8 %reduce-precision_convert_fusion.7 = bf16[1024,2048]{1,0:T(8,128)(2,1)} fusion(bf16[2048,1024]{1,0:T(8,128)(2,1)} %get-tuple-element.62, bf16[2048,2048]{1,0:T(8,128)(2,1)} %get-tuple-element.26), kind=kOutput, calls=%fused_computation.25 | convolution fusion | flops 8594128896 | bytes 16777216 | tf_op jit(solution)/shard_map/dot_general | solution.py:22
  395.1 11.7 %fusion.58 = f32[2048,2048]{1,0:T(8,128)} fusion(bf16[2048,1024]{1,0:T(8,128)(2,1)S(1)} %copy-done.41, bf16[1024,2048]{1,0:T(8,128)(2,1)S(1)} %copy-done.40), kind=kOutput, calls=%fused_computation.147 | convolution fusion | flops 8589934592 | bytes 25165824 | tf_op jit(solution)/shard_map/dot_general | solution.py:34
  406.8 11.7 %reduce-precision_convert_fusion.1 = bf16[2048,2048]{1,0:T(8,128)(2,1)} fusion(f32[2048,2048]{1,0:T(8,128)} %fusion.58, bf16[2048,256]{1,0:T(8,128)(2,1)S(1)} %bitcast.188, bf16[2048,256]{1,0:T(8,128)(2,1)S(1)} %bitcast.212), kind=kOutput, calls=%fused_computation.7 | convolution fusion | flops 2160066560 | bytes 27262976 | tf_op jit(solution)/shard_map/dot_general | solution.py:28
  418.5 14.7 %reduce-precision_convert_fusion.4 = bf16[1024,2048]{1,0:T(8,128)(2,1)} fusion(bf16[2048,1024]{1,0:T(8,128)(2,1)} %get-tuple-element.59, bf16[2048,2048]{1,0:T(8,128)(2,1)} %bitcast.173), kind=kOutput, calls=%fused_computation.21 | convolution fusion | flops 8594128896 | bytes 16777216 | tf_op jit(solution)/shard_map/dot_general | solution.py:22
  442.8 8.3 reduce-precision_convert_fusion.10
  454.0 30.2 %collective-permute-done.6 = bf16[1024,2048]{1,0:T(8,128)(2,1)} collective-permute-done((bf16[1024,2048]{1,0:T(8,128)(2,1)}, bf16[1024,2048]{1,0:T(8,128)(2,1)}, u32[]{:S(2)}, u32[]{:S(2)}) %collective-permute-start.6) | collective-permute-done | bytes 4194336 | tf_op jit(solution)/shard_map/ppermute | solution.py:138
  484.3 7.9 reduce-precision_convert_fusion.6
  501.8 72.4 %collective-permute-done.9 = bf16[1024,2048]{1,0:T(8,128)(2,1)} collective-permute-done((bf16[1024,2048]{1,0:T(8,128)(2,1)}, bf16[1024,2048]{1,0:T(8,128)(2,1)}, u32[]{:S(2)}, u32[]{:S(2)}) %collective-permute-start.9) | collective-permute-done | bytes 4194336 | tf_op jit(solution)/shard_map/ppermute | solution.py:138
  584.6 56.3 %collective-permute-done = bf16[768,2048]{1,0:T(8,128)(2,1)} collective-permute-done((bf16[768,2048]{1,0:T(8,128)(2,1)}, bf16[768,2048]{1,0:T(8,128)(2,1)}, u32[]{:S(2)}, u32[]{:S(2)}) %collective-permute-start) | collective-permute-done | bytes 3145760 | tf_op jit(solution)/shard_map/ppermute | solution.py:138
  655.6 20.9 %collective-permute-done.3 = bf16[256,2048]{1,0:T(8,128)(2,1)S(1)} collective-permute-done((bf16[256,2048]{1,0:T(8,128)(2,1)S(1)}, bf16[256,2048]{1,0:T(8,128)(2,1)S(1)}, u32[]{:S(2)}, u32[]{:S(2)}) %collective-permute-start.3) | collective-permute-done | bytes 1048608 | tf_op jit(solution)/shard_map/ppermute | solution.py:138
  697.3 63.8 %all-to-all-start.7 = ((bf16[2,128,2048]{2,0,1:T(2,128)(2,1)}), bf16[2,128,2048]{2,0,1:T(2,128)(2,1)}, u32[]{:S(2)}, u32[]{:S(2)}) async-start(bf16[2,128,2048]{2,0,1:T(2,128)(2,1)} %copy.202), calls=%async_computation.9 | async-start | bytes 2097152 | tf_op jit(solution)/shard_map/all_to_all | solution.py:192
  777.8 89.9 %all-to-all-done.7 = bf16[2,128,2048]{2,0,1:T(2,128)(2,1)} async-done(((bf16[2,128,2048]{2,0,1:T(2,128)(2,1)}), bf16[2,128,2048]{2,0,1:T(2,128)(2,1)}, u32[]{:S(2)}, u32[]{:S(2)}) %all-to-all-start.7) | async-done | bytes 1048608 | tf_op jit(solution)/shard_map/all_to_all | solution.py:192
  878.6 126.6 %all-reduce.1 = (f32[256,4]{0,1:T(4,128)S(1)}, f32[768]{0:T(1024)}, f32[256]{0:T(256)S(1)}, f32[1024]{0:T(1024)}) all-reduce(f32[256,4]{0,1:T(4,128)S(1)} %copy.219, f32[768]{0:T(1024)S(1)} %convert_reduce_fusion.3, f32[256]{0:T(256)S(1)} %dynamic_slice.15, f32[1024]{0:T(1024)S(1)} %copy-done.37), channel_id=1, replica_groups=mesh['fsdp'=8,'sp'=4] {'sp'}, use_global_device_ids=true, to_apply=%region_18.19 | all-reduce | flops 3072 | bytes 24576 | tf_op jit(solution)/shard_map/psum | solution.py:284
  (242 shorter events, 302.8 us)
Async XLA Ops:
  7.2 212.3 %copy-start = (bf16[768,2048]{1,0:T(8,128)(2,1)S(1)}, bf16[768,2048]{1,0:T(8,128)(2,1)}, u32[]{:S(2)}) copy-start(bf16[768,2048]{1,0:T(8,128)(2,1)} %param.21) | copy-start | bytes 9437188
  7.2 195.9 %all-gather.4.cloned.1.call-start = ((), (), s32[]{:S(2)}) async-start(), calls=%async_computation.13 | async-start | bytes 9437184 | tf_op jit(solution)/shard_map/all_gather | solution.py:187
  83.5 147.9 %all-gather.6.cloned.1.call-start = ((), (), s32[]{:S(2)}) async-start(), calls=%async_computation.15 | async-start | bytes 9437184 | tf_op jit(solution)/shard_map/all_gather | solution.py:187
  164.4 36.5 %all-to-all-start.2 = ((bf16[256,8,256]{0,2,1:T(8,128)(2,1)}), bf16[256,8,256]{0,2,1:T(8,128)(2,1)}, u32[]{:S(2)}, u32[]{:S(2)}) async-start(bf16[256,8,256]{0,2,1:T(8,128)(2,1)} %bitcast.204), calls=%async_computation.2 | async-start | bytes 2097152 | tf_op jit(solution)/shard_map/all_to_all | solution.py:222
  168.7 525.4 %reduce-scatter.8.cloned.1.call-start = ((), (), s32[]{:S(2)}) async-start(), calls=%async_computation.16 | async-start | bytes 9437184 | tf_op jit(solution)/shard_map/reduce_scatter | solution.py:191
  363.8 410.5 %reduce-scatter.6.cloned.1.call-start = ((), (), s32[]{:S(2)}) async-start(), calls=%async_computation.14 | async-start | bytes 9437184 | tf_op jit(solution)/shard_map/reduce_scatter | solution.py:191
  389.4 94.8 %collective-permute-start.6 = (bf16[1024,2048]{1,0:T(8,128)(2,1)}, bf16[1024,2048]{1,0:T(8,128)(2,1)}, u32[]{:S(2)}, u32[]{:S(2)}) collective-permute-start(bf16[1024,2048]{1,0:T(8,128)(2,1)} %reduce-precision_convert_fusion.7), channel_id=1, source_target_pairs={{0,1},{3,2},{4,5},{7,6},{8,9},{11,10},{12,13},{15,14},{16,17},{19,... | collective-permute-start | bytes 12582920 | tf_op jit(solution)/shard_map/ppermute | solution.py:138
  433.2 140.9 %collective-permute-start.9 = (bf16[1024,2048]{1,0:T(8,128)(2,1)}, bf16[1024,2048]{1,0:T(8,128)(2,1)}, u32[]{:S(2)}, u32[]{:S(2)}) collective-permute-start(bf16[1024,2048]{1,0:T(8,128)(2,1)} %reduce-precision_convert_fusion.4), channel_id=1, source_target_pairs={{0,1},{3,2},{4,5},{7,6},{8,9},{11,10},{12,13},{15,14},{16,17},{19,... | collective-permute-start | bytes 12582920 | tf_op jit(solution)/shard_map/ppermute | solution.py:138
  451.1 189.8 %collective-permute-start = (bf16[768,2048]{1,0:T(8,128)(2,1)}, bf16[768,2048]{1,0:T(8,128)(2,1)}, u32[]{:S(2)}, u32[]{:S(2)}) collective-permute-start(bf16[768,2048]{1,0:T(8,128)(2,1)} %reduce-precision_convert_fusion.10), channel_id=1, source_target_pairs={{0,1},{3,2},{4,5},{7,6},{8,9},{11,10},{12,13},{15,14},{16,17},{19,... | collective-permute-start | bytes 9437192 | tf_op jit(solution)/shard_map/ppermute | solution.py:138
  492.1 185.5 %collective-permute-start.7 = (bf16[1024,2048]{1,0:T(8,128)(2,1)}, bf16[1024,2048]{1,0:T(8,128)(2,1)}, u32[]{:S(2)}, u32[]{:S(2)}) collective-permute-start(bf16[1024,2048]{1,0:T(8,128)(2,1)} %reduce-precision_convert_fusion.6), channel_id=1, source_target_pairs={{1,2},{2,1},{5,6},{6,5},{9,10},{10,9},{13,14},{14,13},{17,18},{18,... | collective-permute-start | bytes 12582920 | tf_op jit(solution)/shard_map/ppermute | solution.py:140
  498.2 151.1 %all-to-all-start.9 = ((bf16[8,256,256]{1,2,0:T(8,128)(2,1)}), bf16[8,256,256]{1,2,0:T(8,128)(2,1)S(1)}, u32[]{:S(2)}, u32[]{:S(2)}) async-start(bf16[8,256,256]{1,2,0:T(8,128)(2,1)} %bitcast.164), calls=%async_computation.11 | async-start | bytes 2097152 | tf_op jit(solution)/shard_map/all_to_all | solution.py:270
  581.8 179.4 %collective-permute-start.10 = (bf16[1024,2048]{1,0:T(8,128)(2,1)}, bf16[1024,2048]{1,0:T(8,128)(2,1)}, u32[]{:S(2)}, u32[]{:S(2)}) collective-permute-start(bf16[1024,2048]{1,0:T(8,128)(2,1)} %reduce-precision_convert_fusion.3), channel_id=1, source_target_pairs={{1,2},{2,1},{5,6},{6,5},{9,10},{10,9},{13,14},{14,13},{17,18},{18,... | collective-permute-start | bytes 12582920 | tf_op jit(solution)/shard_map/ppermute | solution.py:140
  647.0 39.6 %collective-permute-start.1 = (bf16[768,2048]{1,0:T(8,128)(2,1)}, bf16[768,2048]{1,0:T(8,128)(2,1)}, u32[]{:S(2)}, u32[]{:S(2)}) collective-permute-start(bf16[768,2048]{1,0:T(8,128)(2,1)} %reduce-precision_convert_fusion.9), channel_id=1, source_target_pairs={{1,2},{2,1},{5,6},{6,5},{9,10},{10,9},{13,14},{14,13},{17,18},{18,... | collective-permute-start | bytes 9437192 | tf_op jit(solution)/shard_map/ppermute | solution.py:140
  650.1 26.4 %collective-permute-start.3 = (bf16[256,2048]{1,0:T(8,128)(2,1)S(1)}, bf16[256,2048]{1,0:T(8,128)(2,1)S(1)}, u32[]{:S(2)}, u32[]{:S(2)}) collective-permute-start(bf16[256,2048]{1,0:T(8,128)(2,1)S(1)} %copy.206), channel_id=1, source_target_pairs={{0,1},{3,2},{4,5},{7,6},{8,9},{11,10},{12,13},{15,14},{16,17},{19,... | collective-permute-start | bytes 3145736 | tf_op jit(solution)/shard_map/ppermute | solution.py:138
  676.9 93.4 %collective-permute-start.4 = (bf16[256,2048]{1,0:T(8,128)(2,1)S(1)}, bf16[256,2048]{1,0:T(8,128)(2,1)S(1)}, u32[]{:S(2)}, u32[]{:S(2)}) collective-permute-start(bf16[256,2048]{1,0:T(8,128)(2,1)S(1)} %reduce-precision_convert_fusion.12), channel_id=1, source_target_pairs={{1,2},{2,1},{5,6},{6,5},{9,10},{10,9},{13,14},{14,13},{17,18},{18,... | collective-permute-start | bytes 3145736 | tf_op jit(solution)/shard_map/ppermute | solution.py:140
  685.3 334.4 %collective-permute-start.8 = (bf16[1024,2048]{1,0:T(8,128)(2,1)}, bf16[1024,2048]{1,0:T(8,128)(2,1)}, u32[]{:S(2)}, u32[]{:S(2)}) collective-permute-start(bf16[1024,2048]{1,0:T(8,128)(2,1)} %reduce-precision_convert_fusion.5), channel_id=1, source_target_pairs={{1,0},{2,3},{5,4},{6,7},{9,8},{10,11},{13,12},{14,15},{17,16},{18,... | collective-permute-start | bytes 12582920 | tf_op jit(solution)/shard_map/ppermute | solution.py:142
  692.7 322.0 %collective-permute-start.2 = (bf16[768,2048]{1,0:T(8,128)(2,1)}, bf16[768,2048]{1,0:T(8,128)(2,1)}, u32[]{:S(2)}, u32[]{:S(2)}) collective-permute-start(bf16[768,2048]{1,0:T(8,128)(2,1)} %reduce-precision_convert_fusion.8), channel_id=1, source_target_pairs={{1,0},{2,3},{5,4},{6,7},{9,8},{10,11},{13,12},{14,15},{17,16},{18,... | collective-permute-start | bytes 9437192 | tf_op jit(solution)/shard_map/ppermute | solution.py:142
  697.3 170.4 %all-to-all-start.7 = ((bf16[2,128,2048]{2,0,1:T(2,128)(2,1)}), bf16[2,128,2048]{2,0,1:T(2,128)(2,1)}, u32[]{:S(2)}, u32[]{:S(2)}) async-start(bf16[2,128,2048]{2,0,1:T(2,128)(2,1)} %copy.202), calls=%async_computation.9 | async-start | bytes 2097152 | tf_op jit(solution)/shard_map/all_to_all | solution.py:192
  761.1 116.5 %reduce-scatter.10.cloned.1.call-start = ((), (), s32[]{:S(2)}) async-start(), calls=%async_computation.17 | async-start | bytes 1179648
  768.9 265.4 %collective-permute-start.11 = (bf16[1024,2048]{1,0:T(8,128)(2,1)}, bf16[1024,2048]{1,0:T(8,128)(2,1)}, u32[]{:S(2)}, u32[]{:S(2)}) collective-permute-start(bf16[1024,2048]{1,0:T(8,128)(2,1)} %reduce-precision_convert_fusion.2), channel_id=1, source_target_pairs={{1,0},{2,3},{5,4},{6,7},{9,8},{10,11},{13,12},{14,15},{17,16},{18,... | collective-permute-start | bytes 12582920 | tf_op jit(solution)/shard_map/ppermute | solution.py:142
  771.6 234.2 %collective-permute-start.5 = (bf16[256,2048]{1,0:T(8,128)(2,1)}, bf16[256,2048]{1,0:T(8,128)(2,1)}, u32[]{:S(2)}, u32[]{:S(2)}) collective-permute-start(bf16[256,2048]{1,0:T(8,128)(2,1)} %reduce-precision_convert_fusion.11), channel_id=1, source_target_pairs={{1,0},{2,3},{5,4},{6,7},{9,8},{10,11},{13,12},{14,15},{17,16},{18,... | collective-permute-start | bytes 3145736 | tf_op jit(solution)/shard_map/ppermute | solution.py:142
  867.7 143.4 %all-to-all-start.3 = ((bf16[2,128,2048]{2,0,1:T(2,128)(2,1)}), bf16[2,128,2048]{2,0,1:T(2,128)(2,1)}, u32[]{:S(2)}, u32[]{:S(2)}) async-start(bf16[2,128,2048]{2,0,1:T(2,128)(2,1)} %copy.186), calls=%async_computation.4 | async-start | bytes 2097152 | tf_op jit(solution)/shard_map/all_to_all | solution.py:192
  1011.2 18.9 %all-to-all-start.8 = ((bf16[8,32,2048]{2,1,0:T(8,128)(2,1)}), bf16[8,32,2048]{2,1,0:T(8,128)(2,1)S(1)}, u32[]{:S(2)}, u32[]{:S(2)}) async-start(bf16[8,32,2048]{2,1,0:T(8,128)(2,1)} %bitcast.55), calls=%async_computation.10 | async-start | bytes 2097152 | tf_op jit(solution)/shard_map/all_to_all | solution.py:193
  1030.1 19.7 %all-to-all-start.4 = ((bf16[8,32,2048]{2,1,0:T(8,128)(2,1)}), bf16[8,32,2048]{2,1,0:T(8,128)(2,1)}, u32[]{:S(2)}, u32[]{:S(2)}) async-start(bf16[8,32,2048]{2,1,0:T(8,128)(2,1)} %bitcast.27), calls=%async_computation.5 | async-start | bytes 2097152 | tf_op jit(solution)/shard_map/all_to_all | solution.py:193
  (45 other events, 680.8 us)
Sparse Core Ops, SparseCore 0:
  83.7 59.1 all-gather.3
  162.2 62.2 all-gather.5
  364.0 71.4 reduce-scatter.7
  439.7 78.5 reduce-scatter.5
  774.4 44.9 reduce-scatter.9
where the time goes:
time: 1070 us; the launch traced here: 1060 us
  waiting for transfers between devices  276 us (26%)
  blocking collectives  257 us (24%)
  matrix products  168 us (16%)
  other arithmetic  151 us (14%)
  starting transfers between devices  115 us (11%)
  local copies, waits for them, and re-layouts  79.8 us (7%)
  between operations  15.1 us (1%)
    ppermute x4, waiting for transfers between devices, sum_over_line(): inward = lax.ppermute(partial, 'sp', [(0, 1), (3, 2)])  180 us
    psum x1, blocking collectives, per_device(): lax.psum((vectors, bias_out, bias_qkv, bias_up), 'sp')  127 us
    all_to_all x2, waiting for transfers between devices, scatter_tokens(): part = lax.all_to_all(part, 'sp', split_axis=1, concat_axis=0, tiled=True)  89.9 us
    all_to_all x2, starting transfers between devices, scatter_tokens(): part = lax.all_to_all(part, 'sp', split_axis=1, concat_axis=0, tiled=True)  68.4 us
    all_to_all x2, blocking collectives, gather_tokens(): part = lax.all_to_all(part, 'sp', split_axis=0, concat_axis=1, tiled=True)  56.6 us
    dot_general x4, matrix products, times_transposed(): lax.dot_general(former, latter, (((1,), (1,)), ((), ())), preferred_eleme...  52 us
    dot_general x4, matrix products, times(): return jnp.dot(former, latter, preferred_element_type=jnp.float32)  49.7 us
    all_to_all x2, blocking collectives, gather_tokens(): lax.all_to_all(block, 'fsdp', split_axis=1, concat_axis=0, tiled=True)  47.4 us
  transfers between devices with their start and end apart: 23, of which 7 were waited for; matrix products, arithmetic and copies ran while one was open for 22% of the time, Pallas kernels for 0%

commit v1 on v0

--- a/solution.py
+++ b/solution.py
@@ -12,6 +12,17 @@
 ROOT_HALF = 0.7071067811865476
 ROOT_TWO_PI = 2.5066282746310002
 SCALE = 1.0 / math.sqrt(HEAD_DIM)
+
+
+def split_up(x, dim, size):
+    before, after = (x.shape[:dim], x.shape[dim + 1 :])
+    return jnp.moveaxis(x.reshape(*before, size, -1, *after), dim, 0)
+
+
+def in_order_2(pieces, dim):
+    lengths = list(pieces.shape[1:])
+    lengths[dim] *= pieces.shape[0]
+    return jnp.moveaxis(pieces, 0, dim).reshape(lengths)
 
 
 def rounded(array):
@@ -183,7 +194,14 @@
 
     def gather_tokens(block):
         part = lax.all_to_all(block, "fsdp", split_axis=1, concat_axis=0, tiled=True)
-        part = lax.all_to_all(part, "sp", split_axis=0, concat_axis=1, tiled=True)
+        count, mine = (lax.axis_size("sp"), lax.axis_index("sp"))
+        blocks = split_up(part, 0, count)
+        outs = [blocks[mine]]
+        for hop in range(1, count):
+            sent = blocks[mine ^ hop]
+            outs.append(lax.ppermute(sent, "sp", [(i, i ^ hop) for i in range(count)]))
+        blocks = jnp.stack(outs)[mine ^ jnp.arange(count)]
+        part = in_order_2(blocks, 1)
         return lax.all_gather(part, "fsdp", axis=0, tiled=True).reshape(tokens, width)
 
     def scatter_tokens(partial):

time: 1070 us -> 1070 us (level)
  blocking collectives: 257 us -> 176 us
  waiting for transfers between devices: 276 us -> 330 us
  starting transfers between devices: 115 us -> 126 us
    all_to_all x2 -> x0, blocking collectives: 56.6 us -> none  [gather_tokens(): part = lax.all_to_all(part, 'sp', split_axis=0, concat_axis=1, tiled=True)]
    ppermute x0 -> x6, waiting for transfers between devices: none -> 37.9 us  [gather_tokens(): outs.append(lax.ppermute(sent, 'sp', [(i, i ^ hop) for i in range(count)]))]
    all_to_all x2 -> x1, blocking collectives: 47.4 us -> 20.7 us  [gather_tokens(): lax.all_to_all(block, 'fsdp', split_axis=1, concat_axis=0, tiled=True)]
    all_to_all x0 -> x1, waiting for transfers between devices: none -> 15.5 us  [gather_tokens(): lax.all_to_all(block, 'fsdp', split_axis=1, concat_axis=0, tiled=True)]
    convert_element_type x9 -> x8, other arithmetic: 45 us -> 44.9 us  [rounded(): lax.reduce_precision(array.astype(jnp.float32), 8, 7).astype(jnp.bfloat16)]
  transfers between devices with their start and end apart: 23 -> 30, of which waited for: 7 -> 12; matrix products, arithmetic and copies ran while one was open for 22% -> 23% of each run, Pallas kernels for 0% -> 0%
where the time goes in v1:
time: 1070 us; the launch traced here: 1060 us
  waiting for transfers between devices  330 us (31%)
  blocking collectives  176 us (16%)
  matrix products  170 us (16%)
  other arithmetic  153 us (14%)
  starting transfers between devices  126 us (12%)
  local copies, waits for them, and re-layouts  86.8 us (8%)
  between operations  15.1 us (1%)
    ppermute x4, waiting for transfers between devices, sum_over_line(): inward = lax.ppermute(partial, 'sp', [(0, 1), (3, 2)])  180 us
    psum x1, blocking collectives, per_device(): lax.psum((vectors, bias_out, bias_qkv, bias_up), 'sp')  127 us
    all_to_all x2, waiting for transfers between devices, scatter_tokens(): part = lax.all_to_all(part, 'sp', split_axis=1, concat_axis=0, tiled=True)  90.2 us
    all_to_all x2, starting transfers between devices, scatter_tokens(): part = lax.all_to_all(part, 'sp', split_axis=1, concat_axis=0, tiled=True)  68.4 us
    dot_general x4, matrix products, times_transposed(): lax.dot_general(former, latter, (((1,), (1,)), ((), ())), preferred_eleme...  51.9 us
    dot_general x4, matrix products, times(): return jnp.dot(former, latter, preferred_element_type=jnp.float32)  49.7 us
    convert_element_type x8, other arithmetic, rounded(): lax.reduce_precision(array.astype(jnp.float32), 8, 7).astype(jnp.bfloat16)  44.9 us
    dot_general x4, matrix products, contract_rows(): lax.dot_general(former, latter, (((0,), (0,)), ((), ())), preferred_eleme...  42.1 us
  transfers between devices with their start and end apart: 30, of which 12 were waited for; matrix products, arithmetic and copies ran while one was open for 23% of the time, Pallas kernels for 0%

profile of v1, /device:TPU:0, one launch (start us, length us, event | category | flops | bytes accessed | tf_op | source)
XLA Modules:
  0.0 1056.6 jit_solution(1930040438688394198)
XLA Ops:
  12.0 9.0 reduce.19
  28.9 15.5 %all-to-all-done = bf16[8,2,32768]{2,1,0:T(2,128)(2,1)} async-done(((bf16[8,2,32768]{2,1,0:T(2,128)(2,1)}), bf16[8,2,32768]{2,1,0:T(2,128)(2,1)}, u32[]{:S(2)}, u32[]{:S(2)}) %all-to-all-start) | async-done | bytes 1048608 | tf_op jit(solution)/shard_map/all_to_all | solution.py:196
  63.7 12.1 %collective-permute-done.1 = bf16[2,32,2048]{2,1,0:T(8,128)(2,1)S(1)} collective-permute-done((bf16[2,32,2048]{2,1,0:T(8,128)(2,1)S(1)}, bf16[2,32,2048]{2,1,0:T(8,128)(2,1)S(1)}, u32[]{:S(2)}, u32[]{:S(2)}) %collective-permute-start.1) | collective-permute-done | bytes 262176 | tf_op jit(solution)/shard_map/ppermute | solution.py:202
  86.5 9.0 reduce.20
  98.1 20.7 %all_to_all.104 = bf16[8,2,32768]{2,1,0:T(2,128)(2,1)} all-to-all(bf16[8,2,32768]{2,1,0:T(2,128)(2,1)} %reshape.631), channel_id=1, replica_groups=mesh['fsdp'=8,'sp'=4] {'fsdp'}, dimensions={0} | all-to-all | bytes 2097152 | tf_op jit(solution)/shard_map/all_to_all | solution.py:196
  138.2 12.5 %collective-permute-done.4 = bf16[2,32,2048]{2,1,0:T(8,128)(2,1)S(1)} collective-permute-done((bf16[2,32,2048]{2,1,0:T(8,128)(2,1)S(1)}, bf16[2,32,2048]{2,1,0:T(8,128)(2,1)S(1)}, u32[]{:S(2)}, u32[]{:S(2)}) %collective-permute-start.4) | collective-permute-done | bytes 262176 | tf_op jit(solution)/shard_map/ppermute | solution.py:202
  163.5 28.1 %all-gather = s32[8,1,1024]{2,1,0:T(1,128)S(1)} all-gather(s32[1,1,1024]{2,1,0:T(1,128)S(1)} %bitcast.252), channel_id=1, replica_groups=mesh['fsdp'=8,'sp'=4] {'fsdp'}, dimensions={0}, use_global_device_ids=true | all-gather | bytes 36864 | tf_op jit(solution)/shard_map/all_gather | solution.py:238
  295.0 15.7 %multiply_convert_fusion.1 = (bf16[2048,1024]{1,0:T(8,128)(2,1)}, f32[2048,1024]{1,0:T(8,128)}) fusion(f32[1024]{0:T(1024)S(1)} %dynamic_slice.42, bf16[2048,2048]{1,0:T(8,128)(2,1)} %get-tuple-element.26, bf16[1024,2048]{1,0:T(8,128)(2,1)S(1)} %copy-done.39), kind=kOutput, calls=%fused_computation.31 | convolution fusion | flops 8602517504 | bytes 25169920 | tf_op jit(solution)/shard_map/dot_general | solution.py:39
  310.6 17.5 %convert_reduce_fusion.2 = (f32[1024]{0:T(1024)}, bf16[2048,1024]{1,0:T(8,128)(2,1)}) fusion(f32[2048,1024]{1,0:T(8,128)} %get-tuple-element.68, f32[1024]{0:T(1024)S(1)} %dynamic_slice.42, bf16[2048,2048]{1,0:T(8,128)(2,1)S(1)} %bitcast.197, bf16[1024,2048]{1,0:T(8,128)(2,1)} %param.27), kind=kOutput, calls=%fused_computation.24 | convolution fusion | flops 8617196544 | bytes 25174016 | tf_op jit(solution)/shard_map/dot_general | solution.py:39
  328.1 14.1 %fusion.61 = f32[2048,2048]{1,0:T(8,128)} fusion(bf16[2048,1024]{1,0:T(8,128)(2,1)} %get-tuple-element.70, bf16[1024,2048]{1,0:T(8,128)(2,1)S(1)} %copy-done.39), kind=kOutput, calls=%fused_computation.163 | convolution fusion | flops 8589934592 | bytes 25165824 | tf_op jit(solution)/shard_map/dot_general | solution.py:45
  342.2 17.8 %multiply_reduce_fusion.1 = (f32[2048]{0:T(1024)S(1)}, f32[2048]{0:T(1024)S(1)}, f32[2048]{0:T(1024)S(1)}, f32[2048]{0:T(1024)S(1)}, bf16[2048,2048]{1,0:T(8,128)(2,1)}) fusion(bf16[16,128,2048]{2,1,0:T(8,128)(2,1)} %all-gather.4.cloned.1.call-done, f32[2048]{0:T(1024)S(1)} %get-tuple-element.56, f32[2048]{0:T(1024)S(1)} %get-tuple-element.57, ...), kind=kOutput, calls=%fused_computation.7 | convolution fusion | flops 6501163008 | bytes 39911424 | tf_op jit(solution)/shard_map/dot_general | solution.py:45
  361.2 8.2 fusion.31
  370.5 15.4 %reduce-precision_convert_fusion.7 = bf16[1024,2048]{1,0:T(8,128)(2,1)} fusion(bf16[2048,1024]{1,0:T(8,128)(2,1)} %get-tuple-element.70, bf16[2048,2048]{1,0:T(8,128)(2,1)} %get-tuple-element.26), kind=kOutput, calls=%fused_computation.27 | convolution fusion | flops 8594128896 | bytes 16777216 | tf_op jit(solution)/shard_map/dot_general | solution.py:33
  389.2 11.7 %fusion.60 = f32[2048,2048]{1,0:T(8,128)} fusion(bf16[2048,1024]{1,0:T(8,128)(2,1)S(1)} %copy-done.41, bf16[1024,2048]{1,0:T(8,128)(2,1)S(1)} %copy-done.40), kind=kOutput, calls=%fused_computation.162 | convolution fusion | flops 8589934592 | bytes 25165824 | tf_op jit(solution)/shard_map/dot_general | solution.py:45
  400.9 11.7 %reduce-precision_convert_fusion.1 = bf16[2048,2048]{1,0:T(8,128)(2,1)} fusion(f32[2048,2048]{1,0:T(8,128)} %fusion.60, bf16[2048,256]{1,0:T(8,128)(2,1)S(1)} %bitcast.224, bf16[2048,256]{1,0:T(8,128)(2,1)S(1)} %bitcast.223), kind=kOutput, calls=%fused_computation.9 | convolution fusion | flops 2160066560 | bytes 27262976 | tf_op jit(solution)/shard_map/dot_general | solution.py:39
  412.7 14.7 %reduce-precision_convert_fusion.4 = bf16[1024,2048]{1,0:T(8,128)(2,1)} fusion(bf16[2048,1024]{1,0:T(8,128)(2,1)} %get-tuple-element.67, bf16[2048,2048]{1,0:T(8,128)(2,1)} %bitcast.194), kind=kOutput, calls=%fused_computation.23 | convolution fusion | flops 8594128896 | bytes 16777216 | tf_op jit(solution)/shard_map/dot_general | solution.py:33
  436.9 8.3 reduce-precision_convert_fusion.10
  448.3 30.1 %collective-permute-done.12 = bf16[1024,2048]{1,0:T(8,128)(2,1)} collective-permute-done((bf16[1024,2048]{1,0:T(8,128)(2,1)}, bf16[1024,2048]{1,0:T(8,128)(2,1)}, u32[]{:S(2)}, u32[]{:S(2)}) %collective-permute-start.12) | collective-permute-done | bytes 4194336 | tf_op jit(solution)/shard_map/ppermute | solution.py:149
  496.2 72.1 %collective-permute-done.15 = bf16[1024,2048]{1,0:T(8,128)(2,1)} collective-permute-done((bf16[1024,2048]{1,0:T(8,128)(2,1)}, bf16[1024,2048]{1,0:T(8,128)(2,1)}, u32[]{:S(2)}, u32[]{:S(2)}) %collective-permute-start.15) | collective-permute-done | bytes 4194336 | tf_op jit(solution)/shard_map/ppermute | solution.py:149
  578.8 56.5 %collective-permute-done.6 = bf16[768,2048]{1,0:T(8,128)(2,1)} collective-permute-done((bf16[768,2048]{1,0:T(8,128)(2,1)}, bf16[768,2048]{1,0:T(8,128)(2,1)}, u32[]{:S(2)}, u32[]{:S(2)}) %collective-permute-start.6) | collective-permute-done | bytes 3145760 | tf_op jit(solution)/shard_map/ppermute | solution.py:149
  648.9 21.5 %collective-permute-done.9 = bf16[256,2048]{1,0:T(8,128)(2,1)S(1)} collective-permute-done((bf16[256,2048]{1,0:T(8,128)(2,1)S(1)}, bf16[256,2048]{1,0:T(8,128)(2,1)S(1)}, u32[]{:S(2)}, u32[]{:S(2)}) %collective-permute-start.9) | collective-permute-done | bytes 1048608 | tf_op jit(solution)/shard_map/ppermute | solution.py:149
  691.3 63.9 %all-to-all-start.5 = ((bf16[2,128,2048]{2,0,1:T(2,128)(2,1)}), bf16[2,128,2048]{2,0,1:T(2,128)(2,1)}, u32[]{:S(2)}, u32[]{:S(2)}) async-start(bf16[2,128,2048]{2,0,1:T(2,128)(2,1)} %copy.195), calls=%async_computation.7 | async-start | bytes 2097152 | tf_op jit(solution)/shard_map/all_to_all | solution.py:210
  771.9 90.2 %all-to-all-done.5 = bf16[2,128,2048]{2,0,1:T(2,128)(2,1)} async-done(((bf16[2,128,2048]{2,0,1:T(2,128)(2,1)}), bf16[2,128,2048]{2,0,1:T(2,128)(2,1)}, u32[]{:S(2)}, u32[]{:S(2)}) %all-to-all-start.5) | async-done | bytes 1048608 | tf_op jit(solution)/shard_map/all_to_all | solution.py:210
  872.9 126.8 %all-reduce.1 = (f32[256,4]{0,1:T(4,128)S(1)}, f32[768]{0:T(1024)}, f32[256]{0:T(256)S(1)}, f32[1024]{0:T(1024)}) all-reduce(f32[256,4]{0,1:T(4,128)S(1)} %copy.210, f32[768]{0:T(1024)S(1)} %convert_reduce_fusion.3, f32[256]{0:T(256)S(1)} %dynamic_slice.47, f32[1024]{0:T(1024)S(1)} %copy-done.37), channel_id=1, replica_groups=mesh['fsdp'=8,'sp'=4] {'sp'}, use_global_device_ids=true, to_apply=%region_18.19 | all-reduce | flops 3072 | bytes 24576 | tf_op jit(solution)/shard_map/psum | solution.py:302
  (260 shorter events, 338.4 us)
Async XLA Ops:
  23.6 20.7 %all-to-all-start = ((bf16[8,2,32768]{2,1,0:T(2,128)(2,1)}), bf16[8,2,32768]{2,1,0:T(2,128)(2,1)}, u32[]{:S(2)}, u32[]{:S(2)}) async-start(bf16[8,2,32768]{2,1,0:T(2,128)(2,1)} %reshape.629), calls=%async_computation | async-start | bytes 2097152 | tf_op jit(solution)/shard_map/all_to_all | solution.py:196
  28.8 170.4 %all-gather.4.cloned.1.call-start = ((), (), s32[]{:S(2)}) async-start(), calls=%async_computation.11 | async-start | bytes 9437184 | tf_op jit(solution)/shard_map/all_gather | solution.py:205
  82.1 145.6 %all-gather.6.cloned.1.call-start = ((), (), s32[]{:S(2)}) async-start(), calls=%async_computation.13 | async-start | bytes 9437184 | tf_op jit(solution)/shard_map/all_gather | solution.py:205
  129.2 21.5 %collective-permute-start.4 = (bf16[2,32,2048]{2,1,0:T(8,128)(2,1)S(1)}, bf16[2,32,2048]{2,1,0:T(8,128)(2,1)S(1)}, u32[]{:S(2)}, u32[]{:S(2)}) collective-permute-start(bf16[2,32,2048]{2,1,0:T(8,128)(2,1)S(1)} %get-tuple-element.47), channel_id=1, source_target_pairs={{0,2},{1,3},{2,0},{3,1},{4,6},{5,7},{6,4},{7,5},{8,10},{9,11},{10,... | collective-permute-start | bytes 786440 | tf_op jit(solution)/shard_map/ppermute | solution.py:202
  129.2 21.5 %collective-permute-start.3 = (bf16[2,32,2048]{2,1,0:T(8,128)(2,1)S(1)}, bf16[2,32,2048]{2,1,0:T(8,128)(2,1)S(1)}, u32[]{:S(2)}, u32[]{:S(2)}) collective-permute-start(bf16[2,32,2048]{2,1,0:T(8,128)(2,1)S(1)} %get-tuple-element.48), channel_id=1, source_target_pairs={{0,1},{1,0},{2,3},{3,2},{4,5},{5,4},{6,7},{7,6},{8,9},{9,8},{10,11... | collective-permute-start | bytes 786440 | tf_op jit(solution)/shard_map/ppermute | solution.py:202
  159.2 37.8 %all-to-all-start.1 = ((bf16[256,8,256]{0,2,1:T(8,128)(2,1)}), bf16[256,8,256]{0,2,1:T(8,128)(2,1)}, u32[]{:S(2)}, u32[]{:S(2)}) async-start(bf16[256,8,256]{0,2,1:T(8,128)(2,1)} %bitcast.218), calls=%async_computation.1 | async-start | bytes 2097152 | tf_op jit(solution)/shard_map/all_to_all | solution.py:240
  163.4 524.6 %reduce-scatter.8.cloned.1.call-start = ((), (), s32[]{:S(2)}) async-start(), calls=%async_computation.14 | async-start | bytes 9437184 | tf_op jit(solution)/shard_map/reduce_scatter | solution.py:209
  360.0 408.4 %reduce-scatter.6.cloned.1.call-start = ((), (), s32[]{:S(2)}) async-start(), calls=%async_computation.12 | async-start | bytes 9437184 | tf_op jit(solution)/shard_map/reduce_scatter | solution.py:209
  385.9 92.5 %collective-permute-start.12 = (bf16[1024,2048]{1,0:T(8,128)(2,1)}, bf16[1024,2048]{1,0:T(8,128)(2,1)}, u32[]{:S(2)}, u32[]{:S(2)}) collective-permute-start(bf16[1024,2048]{1,0:T(8,128)(2,1)} %reduce-precision_convert_fusion.7), channel_id=1, source_target_pairs={{0,1},{3,2},{4,5},{7,6},{8,9},{11,10},{12,13},{15,14},{16,17},{19,... | collective-permute-start | bytes 12582920 | tf_op jit(solution)/shard_map/ppermute | solution.py:149
  427.4 140.9 %collective-permute-start.15 = (bf16[1024,2048]{1,0:T(8,128)(2,1)}, bf16[1024,2048]{1,0:T(8,128)(2,1)}, u32[]{:S(2)}, u32[]{:S(2)}) collective-permute-start(bf16[1024,2048]{1,0:T(8,128)(2,1)} %reduce-precision_convert_fusion.4), channel_id=1, source_target_pairs={{0,1},{3,2},{4,5},{7,6},{8,9},{11,10},{12,13},{15,14},{16,17},{19,... | collective-permute-start | bytes 12582920 | tf_op jit(solution)/shard_map/ppermute | solution.py:149
  445.3 190.0 %collective-permute-start.6 = (bf16[768,2048]{1,0:T(8,128)(2,1)}, bf16[768,2048]{1,0:T(8,128)(2,1)}, u32[]{:S(2)}, u32[]{:S(2)}) collective-permute-start(bf16[768,2048]{1,0:T(8,128)(2,1)} %reduce-precision_convert_fusion.10), channel_id=1, source_target_pairs={{0,1},{3,2},{4,5},{7,6},{8,9},{11,10},{12,13},{15,14},{16,17},{19,... | collective-permute-start | bytes 9437192 | tf_op jit(solution)/shard_map/ppermute | solution.py:149
  486.2 185.3 %collective-permute-start.13 = (bf16[1024,2048]{1,0:T(8,128)(2,1)}, bf16[1024,2048]{1,0:T(8,128)(2,1)}, u32[]{:S(2)}, u32[]{:S(2)}) collective-permute-start(bf16[1024,2048]{1,0:T(8,128)(2,1)} %reduce-precision_convert_fusion.6), channel_id=1, source_target_pairs={{1,2},{2,1},{5,6},{6,5},{9,10},{10,9},{13,14},{14,13},{17,18},{18,... | collective-permute-start | bytes 12582920 | tf_op jit(solution)/shard_map/ppermute | solution.py:151
  492.6 151.3 %all-to-all-start.7 = ((bf16[8,256,256]{2,1,0:T(8,128)(2,1)}), bf16[8,256,256]{2,1,0:T(8,128)(2,1)S(1)}, u32[]{:S(2)}, u32[]{:S(2)}) async-start(bf16[8,256,256]{2,1,0:T(8,128)(2,1)} %bitcast.77), calls=%async_computation.9 | async-start | bytes 2097152 | tf_op jit(solution)/shard_map/all_to_all | solution.py:288
  576.0 179.4 %collective-permute-start.16 = (bf16[1024,2048]{1,0:T(8,128)(2,1)}, bf16[1024,2048]{1,0:T(8,128)(2,1)}, u32[]{:S(2)}, u32[]{:S(2)}) collective-permute-start(bf16[1024,2048]{1,0:T(8,128)(2,1)} %reduce-precision_convert_fusion.3), channel_id=1, source_target_pairs={{1,2},{2,1},{5,6},{6,5},{9,10},{10,9},{13,14},{14,13},{17,18},{18,... | collective-permute-start | bytes 12582920 | tf_op jit(solution)/shard_map/ppermute | solution.py:151
  641.4 39.2 %collective-permute-start.7 = (bf16[768,2048]{1,0:T(8,128)(2,1)}, bf16[768,2048]{1,0:T(8,128)(2,1)}, u32[]{:S(2)}, u32[]{:S(2)}) collective-permute-start(bf16[768,2048]{1,0:T(8,128)(2,1)} %reduce-precision_convert_fusion.9), channel_id=1, source_target_pairs={{1,2},{2,1},{5,6},{6,5},{9,10},{10,9},{13,14},{14,13},{17,18},{18,... | collective-permute-start | bytes 9437192 | tf_op jit(solution)/shard_map/ppermute | solution.py:151
  644.1 26.3 %collective-permute-start.9 = (bf16[256,2048]{1,0:T(8,128)(2,1)S(1)}, bf16[256,2048]{1,0:T(8,128)(2,1)S(1)}, u32[]{:S(2)}, u32[]{:S(2)}) collective-permute-start(bf16[256,2048]{1,0:T(8,128)(2,1)S(1)} %bitcast.212), channel_id=1, source_target_pairs={{0,1},{3,2},{4,5},{7,6},{8,9},{11,10},{12,13},{15,14},{16,17},{19,... | collective-permute-start | bytes 3145736 | tf_op jit(solution)/shard_map/ppermute | solution.py:149
  670.8 93.5 %collective-permute-start.10 = (bf16[256,2048]{1,0:T(8,128)(2,1)S(1)}, bf16[256,2048]{1,0:T(8,128)(2,1)S(1)}, u32[]{:S(2)}, u32[]{:S(2)}) collective-permute-start(bf16[256,2048]{1,0:T(8,128)(2,1)S(1)} %reduce-precision_convert_fusion.12), channel_id=1, source_target_pairs={{1,2},{2,1},{5,6},{6,5},{9,10},{10,9},{13,14},{14,13},{17,18},{18,... | collective-permute-start | bytes 3145736 | tf_op jit(solution)/shard_map/ppermute | solution.py:151
  679.3 334.9 %collective-permute-start.14 = (bf16[1024,2048]{1,0:T(8,128)(2,1)}, bf16[1024,2048]{1,0:T(8,128)(2,1)}, u32[]{:S(2)}, u32[]{:S(2)}) collective-permute-start(bf16[1024,2048]{1,0:T(8,128)(2,1)} %reduce-precision_convert_fusion.5), channel_id=1, source_target_pairs={{1,0},{2,3},{5,4},{6,7},{9,8},{10,11},{13,12},{14,15},{17,16},{18,... | collective-permute-start | bytes 12582920 | tf_op jit(solution)/shard_map/ppermute | solution.py:153
  686.7 322.5 %collective-permute-start.8 = (bf16[768,2048]{1,0:T(8,128)(2,1)}, bf16[768,2048]{1,0:T(8,128)(2,1)}, u32[]{:S(2)}, u32[]{:S(2)}) collective-permute-start(bf16[768,2048]{1,0:T(8,128)(2,1)} %reduce-precision_convert_fusion.8), channel_id=1, source_target_pairs={{1,0},{2,3},{5,4},{6,7},{9,8},{10,11},{13,12},{14,15},{17,16},{18,... | collective-permute-start | bytes 9437192 | tf_op jit(solution)/shard_map/ppermute | solution.py:153
  691.3 170.7 %all-to-all-start.5 = ((bf16[2,128,2048]{2,0,1:T(2,128)(2,1)}), bf16[2,128,2048]{2,0,1:T(2,128)(2,1)}, u32[]{:S(2)}, u32[]{:S(2)}) async-start(bf16[2,128,2048]{2,0,1:T(2,128)(2,1)} %copy.195), calls=%async_computation.7 | async-start | bytes 2097152 | tf_op jit(solution)/shard_map/all_to_all | solution.py:210
  755.3 116.7 %reduce-scatter.10.cloned.1.call-start = ((), (), s32[]{:S(2)}) async-start(), calls=%async_computation.15 | async-start | bytes 1179648
  763.0 265.8 %collective-permute-start.17 = (bf16[1024,2048]{1,0:T(8,128)(2,1)}, bf16[1024,2048]{1,0:T(8,128)(2,1)}, u32[]{:S(2)}, u32[]{:S(2)}) collective-permute-start(bf16[1024,2048]{1,0:T(8,128)(2,1)} %reduce-precision_convert_fusion.2), channel_id=1, source_target_pairs={{1,0},{2,3},{5,4},{6,7},{9,8},{10,11},{13,12},{14,15},{17,16},{18,... | collective-permute-start | bytes 12582920 | tf_op jit(solution)/shard_map/ppermute | solution.py:153
  765.7 234.6 %collective-permute-start.11 = (bf16[256,2048]{1,0:T(8,128)(2,1)}, bf16[256,2048]{1,0:T(8,128)(2,1)}, u32[]{:S(2)}, u32[]{:S(2)}) collective-permute-start(bf16[256,2048]{1,0:T(8,128)(2,1)} %reduce-precision_convert_fusion.11), channel_id=1, source_target_pairs={{1,0},{2,3},{5,4},{6,7},{9,8},{10,11},{13,12},{14,15},{17,16},{18,... | collective-permute-start | bytes 3145736 | tf_op jit(solution)/shard_map/ppermute | solution.py:153
  862.1 143.6 %all-to-all-start.2 = ((bf16[2,128,2048]{2,0,1:T(2,128)(2,1)}), bf16[2,128,2048]{2,0,1:T(2,128)(2,1)}, u32[]{:S(2)}, u32[]{:S(2)}) async-start(bf16[2,128,2048]{2,0,1:T(2,128)(2,1)} %copy.179), calls=%async_computation.3 | async-start | bytes 2097152 | tf_op jit(solution)/shard_map/all_to_all | solution.py:210
  (52 other events, 983.1 us)
Sparse Core Ops, SparseCore 0:
  82.2 60.9 all-gather.3
  157.0 63.3 all-gather.5
  360.2 69.6 reduce-scatter.7
  434.2 78.6 reduce-scatter.5
  768.5 44.9 reduce-scatter.9
